TPU v7x, 256 devices: a whole 4x4x8 slice. The times are simulated.
256 devices in a mesh: seq: 32 (over x, y, core), head: 8 (over z).
Axes of the slice: x: 4, y: 4, z: 8, core: 2. Of those that a mesh axis runs over, the one named last changes fastest.
Arguments:
- queries: bfloat16 [32768, 64, 128], P(('seq', 'head')), may hold values from -8 to 8
- keys: bfloat16 [32768, 8, 128], P(('seq', 'head')), may hold values from -8 to 8
- values: bfloat16 [32768, 8, 128], P(('seq', 'head')), may hold values from -6 to 6
- ancestors: int32 [256, 8], P('seq'), may hold values from 0 to 255, as said below
- lengths: int32 [256], replicated, may hold values from 2 to 128
Outputs:
- attended: bfloat16 [32768, 64, 128], P(('seq', 'head'))
Inputs may be any that keep to these rules, and one draw needn't show every extreme that they name: The 8 ancestors of a block are distinct blocks held on other indices of seq; the blocks of one index of seq name, all together, exactly 2 distinct blocks of each of 6 other indices and no other block.
All inputs are finite; a program needn't handle non-finite values.
Results may differ from a plain program's by a relative error of at most 0.0049.
Values may be sent and summed in bfloat16 or wider, within the bound.
No kernel may reach another device: no remote copies, remote signals or barrier semaphores. Data moves between devices by JAX's collectives and lax.ppermute only.
A program may use at most 64 MiB of HBM per device.

v0:
```python
import math
import jax
import jax.numpy as jnp
from jax import lax
from jax.sharding import PartitionSpec as P

BS = 128
negative_fill = -1e30


def attend_block(query_block, key_self, value_self, key_far, value_far, length_self, length_far):
    width = query_block.shape[-1]
    block_rows = key_self.shape[0]
    kv_groups = key_self.shape[1]
    far_count = key_far.shape[0]
    key_all = jnp.concatenate([key_self[None], key_far], axis=0).reshape(-1, kv_groups, width)
    value_all = jnp.concatenate([value_self[None], value_far], axis=0).reshape(-1, kv_groups, width)
    scores = jnp.einsum("tgsd,kgd->gstk", query_block, key_all, preferred_element_type=jnp.float32)
    scores = scores * (1.0 / math.sqrt(width))
    offsets_row = jnp.arange(block_rows, dtype=jnp.int32)
    self_mask = (offsets_row[None, :] <= offsets_row[:, None]) & (
        offsets_row[None, :] < length_self
    )
    far_mask = (offsets_row[None, :] < length_far[:, None]).reshape(1, far_count * block_rows)
    far_mask = jnp.broadcast_to(far_mask, (block_rows, far_count * block_rows))
    allowed = jnp.concatenate([self_mask, far_mask], axis=1)
    scores = jnp.where(allowed, scores, negative_fill)
    largest = jnp.max(scores, axis=-1, keepdims=True)
    exponent = jnp.exp(scores - largest)
    weights = (exponent / jnp.sum(exponent, axis=-1, keepdims=True)).astype(jnp.bfloat16)
    mixed = jnp.einsum("gstk,kgd->tgsd", weights, value_all, preferred_element_type=jnp.float32)
    return mixed.astype(jnp.bfloat16)


def attend_items(items):
    query_block, key_self, value_self, key_far, value_far, length_self, length_far = items
    return attend_block(
        query_block, key_self, value_self, key_far, value_far, length_self, length_far
    )


def local(queries, keys, values, ancestors, lengths):
    query_local, key_local, value_local = (
        lax.all_to_all(queries, "head", split_axis=1, concat_axis=0, tiled=True),
        lax.all_to_all(keys, "head", split_axis=1, concat_axis=0, tiled=True),
        lax.all_to_all(values, "head", split_axis=1, concat_axis=0, tiled=True),
    )
    token_rows, head_count, width = query_local.shape
    kv_groups = key_local.shape[1]
    blk_dev = token_rows // BS
    seq_place = lax.axis_index("seq")
    key_blocks = key_local.reshape(blk_dev, BS, kv_groups, width)
    value_blocks = value_local.reshape(blk_dev, BS, kv_groups, width)
    key_every, value_every = (
        lax.all_gather(key_local, "seq", axis=0, tiled=True),
        lax.all_gather(value_local, "seq", axis=0, tiled=True),
    )
    key_every = key_every.reshape(-1, BS, kv_groups, width)
    value_every = value_every.reshape(-1, BS, kv_groups, width)
    key_far = jnp.take(key_every, ancestors, axis=0)
    value_far = jnp.take(value_every, ancestors, axis=0)
    length_self = lax.dynamic_slice_in_dim(lengths, seq_place * blk_dev, blk_dev)
    length_far = jnp.take(lengths, ancestors, axis=0)
    query_blocks = query_local.reshape(blk_dev, BS, kv_groups, head_count // kv_groups, width)
    mixed = lax.map(
        attend_items,
        (query_blocks, key_blocks, value_blocks, key_far, value_far, length_self, length_far),
    )
    mixed = mixed.reshape(token_rows, head_count, width)
    return lax.all_to_all(mixed, "head", split_axis=0, concat_axis=1, tiled=True)


def solution(mesh):
    placed = (
        P(("seq", "head"), None, None),
        P(("seq", "head"), None, None),
        P(("seq", "head"), None, None),
        P("seq", None),
        P(),
    )
    return jax.shard_map(
        local, mesh=mesh, in_specs=placed, out_specs=P(("seq", "head"), None, None), check_vma=False
    )
```

profile of v0, /device:TPU:1, one launch (start us, length us, event | category | flops | bytes accessed | tf_op | source)
XLA Modules:
  0.0 284.1 jit_solution(3996163437452136307)
XLA Ops:
  6.5 1.1 copy.28
  7.7 19.4 %all_to_all.69 = bf16[128,8,128]{2,0,1:T(8,128)(2,1)} all-to-all(bf16[128,8,128]{2,0,1:T(8,128)(2,1)S(1)} %copy.28), channel_id=1, replica_groups=mesh['seq'=32,'head'=8] {'head'}, dimensions={1} | all-to-all | bytes 524288 | tf_op jit(solution)/shard_map/all_to_all | solution.py:45
  27.2 1.0 copy.27
  28.1 12.5 %all_to_all.70 = bf16[128,8,128]{2,0,1:T(8,128)(2,1)} all-to-all(bf16[128,8,128]{2,0,1:T(8,128)(2,1)S(1)} %copy.27), channel_id=1, replica_groups=mesh['seq'=32,'head'=8] {'head'}, dimensions={1} | all-to-all | bytes 524288 | tf_op jit(solution)/shard_map/all_to_all | solution.py:46
  40.7 2.7 copy.29
  43.4 4.5 %all-to-all-start.2 = ((bf16[128,64,128]{2,0,1:T(8,128)(2,1)}), bf16[128,64,128]{2,0,1:T(8,128)(2,1)}, u32[]{:S(2)}, u32[]{:S(2)}) async-start(bf16[128,64,128]{2,0,1:T(8,128)(2,1)} %copy.29), calls=%async_computation.2 | async-start | bytes 4194304 | tf_op jit(solution)/shard_map/all_to_all | solution.py:44
  48.1 0.8 gather_fusion
  48.9 34.5 %all-gather.5.cloned.1.call-done = bf16[32768,1,128]{2,0,1:T(8,128)(2,1)} async-done(((bf16[1024,1,128]{2,0,1:T(8,128)(2,1)}), bf16[32768,1,128]{2,0,1:T(8,128)(2,1)}) %all-gather.5.cloned.1.call-update) | async-done | bytes 8388624 | tf_op jit(solution)/shard_map/all_gather | solution.py:55
  83.5 4.3 %gather_fusion.2 = bf16[64,128,128]{2,1,0:T(8,128)(2,1)S(1)} fusion(bf16[256,128,128]{2,1,0:T(8,128)(2,1)} %bitcast.124, s32[1024]{0:T(1024)S(1)} %pad_clamp_fusion), kind=kCustom, calls=%fused_computation.1.clone | custom fusion | bytes 4194560 | tf_op jit(solution)/shard_map/jit(_take)/gather | solution.py:60
  87.8 55.7 %all-gather.3.cloned.1.call-done = bf16[32768,1,128]{2,0,1:T(8,128)(2,1)} async-done(((bf16[1024,1,128]{2,0,1:T(8,128)(2,1)}), bf16[32768,1,128]{2,0,1:T(8,128)(2,1)}) %all-gather.3.cloned.1.call-update) | async-done | bytes 8388624 | tf_op jit(solution)/shard_map/all_gather | solution.py:56
  143.5 5.6 %gather_fusion.1 = bf16[64,128,128]{2,1,0:T(8,128)(2,1)} fusion(bf16[256,128,128]{2,1,0:T(8,128)(2,1)} %bitcast.125, s32[1024]{0:T(1024)S(1)} %pad_clamp_fusion), kind=kCustom, calls=%fused_computation.clone | custom fusion | bytes 4194560 | tf_op jit(solution)/shard_map/jit(_take)/gather | solution.py:61
  149.1 1.6 broadcast_select_fusion
  150.6 0.8 copy-done.1
  151.7 65.8 %while.10 = (s32[]{:T(128)}, bf16[8,128,1,8,128]{4,3,1,0,2:T(8,128)(2,1)}, bf16[8,128,1,128]{3,1,0,2:T(8,128)(2,1)}, bf16[8,8,128,1,128]{4,2,1,3,0:T(8,128)(2,1)...) while((s32[]{:T(128)}, ...), condition=%wide.region_3.5_spmd, body=%wide.region_0.4_spmd.sunk | while | flops 616381568 | bytes 19325688 | solution.py:65
  153.1 0.8 constant_dynamic-slice_fusion.4
  154.1 1.0 dynamic-slice_bitcast_fusion.3
  155.1 1.8 fusion.34
  156.9 0.8 fusion.35
  157.8 1.3 fusion.36
  159.2 0.7 constant_dynamic-update-slice_fusion.2
  161.3 0.8 constant_dynamic-slice_fusion.4
  162.3 1.0 dynamic-slice_bitcast_fusion.3
  163.4 1.8 fusion.34
  165.2 0.8 fusion.35
  166.0 1.3 fusion.36
  167.4 0.7 constant_dynamic-update-slice_fusion.2
  169.5 0.8 constant_dynamic-slice_fusion.4
  170.5 1.0 dynamic-slice_bitcast_fusion.3
  171.6 1.8 fusion.34
  173.4 0.8 fusion.35
  174.2 1.3 fusion.36
  175.7 0.7 constant_dynamic-update-slice_fusion.2
  177.7 0.8 constant_dynamic-slice_fusion.4
  178.8 1.0 dynamic-slice_bitcast_fusion.3
  179.8 1.8 fusion.34
  181.6 0.8 fusion.35
  182.4 1.3 fusion.36
  183.9 0.7 constant_dynamic-update-slice_fusion.2
  186.0 0.8 constant_dynamic-slice_fusion.4
  187.0 1.0 dynamic-slice_bitcast_fusion.3
  188.1 1.8 fusion.34
  189.8 0.8 fusion.35
  190.7 1.3 fusion.36
  192.1 0.7 constant_dynamic-update-slice_fusion.2
  194.2 0.8 constant_dynamic-slice_fusion.4
  195.2 1.0 dynamic-slice_bitcast_fusion.3
  196.3 1.8 fusion.34
  198.1 0.8 fusion.35
  198.9 1.3 fusion.36
  200.3 0.7 constant_dynamic-update-slice_fusion.2
  202.4 0.8 constant_dynamic-slice_fusion.4
  203.4 1.0 dynamic-slice_bitcast_fusion.3
  204.5 1.8 fusion.34
  206.3 0.8 fusion.35
  207.1 1.3 fusion.36
  208.6 0.7 constant_dynamic-update-slice_fusion.2
  210.7 0.8 constant_dynamic-slice_fusion.4
  211.7 1.0 dynamic-slice_bitcast_fusion.3
  212.7 1.8 fusion.34
  214.5 0.8 fusion.35
  215.3 1.3 fusion.36
  216.8 0.7 constant_dynamic-update-slice_fusion.2
  217.5 57.8 %all_to_all.71 = bf16[1024,8,128]{2,1,0:T(8,128)(2,1)S(1)} all-to-all(bf16[1024,8,128]{2,1,0:T(8,128)(2,1)} %bitcast.119), channel_id=1, replica_groups=mesh['seq'=32,'head'=8] {'head'}, dimensions={0} | all-to-all | bytes 4194304 | tf_op jit(solution)/shard_map/all_to_all | solution.py:70
  275.3 1.9 copy.39
  (100 shorter events, 15.0 us)
Async XLA Ops:
  6.5 34.1 %copy-start.2 = (bf16[128,64,128]{2,1,0:T(8,128)(2,1)S(1)}, bf16[128,64,128]{2,1,0:T(8,128)(2,1)}, u32[]{:S(2)}) copy-start(bf16[128,64,128]{2,1,0:T(8,128)(2,1)} %param.9) | copy-start | bytes 6291460
  6.5 76.9 %all-gather.5.cloned.1.call-start = ((), (), s32[]{:S(2)}) async-start(), calls=%async_computation.5 | async-start | bytes 8650752 | tf_op jit(solution)/shard_map/all_gather | solution.py:55
  27.1 116.4 %all-gather.3.cloned.1.call-start = ((), (), s32[]{:S(2)}) async-start(), calls=%async_computation.4 | async-start | bytes 8650752 | tf_op jit(solution)/shard_map/all_gather | solution.py:56
  43.4 4.5 %copy-start.3 = (s32[8,8]{1,0:T(8,128)S(1)}, s32[8,8]{1,0:T(8,128)}, u32[]{:S(2)}) copy-start(s32[8,8]{1,0:T(8,128)} %param.12) | copy-start | bytes 772
  43.4 4.6 %copy-start = (s32[256]{0:T(256)S(1)}, s32[256]{0:T(256)}, u32[]{:S(2)}) copy-start(s32[256]{0:T(256)} %param.13) | copy-start | bytes 3076
  43.4 108.3 %all-to-all-start.2 = ((bf16[128,64,128]{2,0,1:T(8,128)(2,1)}), bf16[128,64,128]{2,0,1:T(8,128)(2,1)}, u32[]{:S(2)}, u32[]{:S(2)}) async-start(bf16[128,64,128]{2,0,1:T(8,128)(2,1)} %copy.29), calls=%async_computation.2 | async-start | bytes 4194304 | tf_op jit(solution)/shard_map/all_to_all | solution.py:44
  149.1 2.3 copy-start.1
Sparse Core Ops, SparseCore 0:
  27.2 56.1 all-gather.4
  86.0 57.4 all-gather.2
where the time goes:
time: 286 us; the launch traced here: 284 us
  waiting for transfers between devices  90.2 us (32%)
  blocking collectives  89.7 us (31%)
  local copies, waits for them, and re-layouts  44.8 us (16%)
  matrix products  24.2 us (8%)
  other arithmetic  16.5 us (6%)
  between operations  13.5 us (5%)
  starting transfers between devices  4.53 us (2%)
    all_to_all x1, blocking collectives, local(): lax.all_to_all(mixed, 'head', split_axis=0, concat_axis=1, tiled=True)  57.8 us
    all_gather x1, waiting for transfers between devices, local(): lax.all_gather(value_local, 'seq', axis=0, tiled=True)  55.7 us
    all_gather x1, waiting for transfers between devices, local(): lax.all_gather(key_local, 'seq', axis=0, tiled=True)  34.5 us
    all_to_all x1, blocking collectives, local(): lax.all_to_all(keys, 'head', split_axis=1, concat_axis=0, tiled=True)  19.4 us
    dot_general x8, matrix products, attend_block(): jnp.einsum('tgsd,kgd->gstk', query_block, key_all, preferred_element_type...  14.2 us
    all_to_all x1, blocking collectives, local(): lax.all_to_all(values, 'head', split_axis=1, concat_axis=0, tiled=True)  12.5 us
    dynamic_slice x16, local copies, waits for them, and re-layouts, local(): lax.map(attend_items, (query_blocks, key_blocks, value_blocks, key_far, v...  11 us
    dot_general x8, matrix products, attend_block(): jnp.einsum('gstk,kgd->tgsd', weights, value_all, preferred_element_type=j...  10 us
  transfers between devices with their start and end apart: 3, of which 2 were waited for; matrix products, arithmetic and copies ran while one was open for 6% of the time, Pallas kernels for 0%

commit v1 on v0

--- a/solution.py
+++ b/solution.py
@@ -40,6 +40,13 @@
 
 
 def local(queries, keys, values, ancestors, lengths):
+
+    def unite_the_goods(payload):
+        block_now = lax.axis_size("seq")
+        n_now = jnp.stack(block_now * [payload], axis=0)
+        extra = lax.all_to_all(n_now, axis_name="seq", split_axis=0, concat_axis=0)
+        return jnp.concatenate(extra, axis=0)
+
     query_local, key_local, value_local = (
         lax.all_to_all(queries, "head", split_axis=1, concat_axis=0, tiled=True),
         lax.all_to_all(keys, "head", split_axis=1, concat_axis=0, tiled=True),
@@ -52,7 +59,7 @@
     key_blocks = key_local.reshape(blk_dev, BS, kv_groups, width)
     value_blocks = value_local.reshape(blk_dev, BS, kv_groups, width)
     key_every, value_every = (
-        lax.all_gather(key_local, "seq", axis=0, tiled=True),
+        unite_the_goods(key_local),
         lax.all_gather(value_local, "seq", axis=0, tiled=True),
     )
     key_every = key_every.reshape(-1, BS, kv_groups, width)

time: 286 us -> 359 us (1.26)
  waiting for transfers between devices: 90.2 us -> 151 us
  starting transfers between devices: 4.53 us -> 14.9 us
  local copies, waits for them, and re-layouts: 44.8 us -> 48.5 us
    all_to_all x0 -> x1, waiting for transfers between devices: none -> 113 us  [unite_the_goods(): extra = lax.all_to_all(n_now, axis_name='seq', split_axis=0, concat_axis=0)]
    all_gather x1, waiting for transfers between devices: 55.7 us -> 0.01 us  [local(): lax.all_gather(value_local, 'seq', axis=0, tiled=True)]
    all_to_all x1, waiting for transfers between devices: 0.01 us -> 37.6 us  [local(): lax.all_to_all(queries, 'head', split_axis=1, concat_axis=0, tiled=True)]
    all_gather x1 -> x0, waiting for transfers between devices: 34.5 us -> none  [local(): lax.all_gather(key_local, 'seq', axis=0, tiled=True)]
    all_to_all x0 -> x1, starting transfers between devices: none -> 10.6 us  [unite_the_goods(): extra = lax.all_to_all(n_now, axis_name='seq', split_axis=0, concat_axis=0)]
    all_to_all x1, blocking collectives: 19.4 us -> 12 us  [local(): lax.all_to_all(keys, 'head', split_axis=1, concat_axis=0, tiled=True)]
    all_to_all x1, blocking collectives: 12.5 us -> 19.4 us  [local(): lax.all_to_all(values, 'head', split_axis=1, concat_axis=0, tiled=True)]
    another operation x0 -> x1, local copies, waits for them, and re-layouts: none -> 5.11 us  [unite_the_goods(): n_now = jnp.stack(block_now * [payload], axis=0)]
where the time goes in v1:
time: 359 us; the launch traced here: 357 us
  waiting for transfers between devices  151 us (42%)
  blocking collectives  86.6 us (24%)
  local copies, waits for them, and re-layouts  48.5 us (14%)
  matrix products  24.2 us (7%)
  other arithmetic  18.3 us (5%)
  starting transfers between devices  14.9 us (4%)
  between operations  13.5 us (4%)
    all_to_all x1, waiting for transfers between devices, unite_the_goods(): extra = lax.all_to_all(n_now, axis_name='seq', split_axis=0, concat_axis=0)  113 us
    all_to_all x1, blocking collectives, local(): lax.all_to_all(mixed, 'head', split_axis=0, concat_axis=1, tiled=True)  55.1 us
    all_to_all x1, waiting for transfers between devices, local(): lax.all_to_all(queries, 'head', split_axis=1, concat_axis=0, tiled=True)  37.6 us
    all_to_all x1, blocking collectives, local(): lax.all_to_all(values, 'head', split_axis=1, concat_axis=0, tiled=True)  19.4 us
    dot_general x8, matrix products, attend_block(): jnp.einsum('tgsd,kgd->gstk', query_block, key_all, preferred_element_type...  14.2 us
    all_to_all x1, blocking collectives, local(): lax.all_to_all(keys, 'head', split_axis=1, concat_axis=0, tiled=True)  12 us
    dynamic_slice x16, local copies, waits for them, and re-layouts, local(): lax.map(attend_items, (query_blocks, key_blocks, value_blocks, key_far, v...  11.1 us
    all_to_all x1, starting transfers between devices, unite_the_goods(): extra = lax.all_to_all(n_now, axis_name='seq', split_axis=0, concat_axis=0)  10.6 us
  transfers between devices with their start and end apart: 3, of which 2 were waited for; matrix products, arithmetic and copies ran while one was open for 6% of the time, Pallas kernels for 0%

profile of v1, /device:TPU:1, one launch (start us, length us, event | category | flops | bytes accessed | tf_op | source)
XLA Modules:
  0.0 357.4 jit_solution(806123503466299249)
XLA Ops:
  6.5 1.0 copy.29
  7.5 19.4 %all_to_all.71 = bf16[128,8,128]{2,0,1:T(8,128)(2,1)} all-to-all(bf16[128,8,128]{2,0,1:T(8,128)(2,1)S(1)} %copy.29), channel_id=1, replica_groups=mesh['seq'=32,'head'=8] {'head'}, dimensions={1} | all-to-all | bytes 524288 | tf_op jit(solution)/shard_map/all_to_all | solution.py:53
  27.0 1.0 copy.30
  27.9 12.0 %all_to_all.72 = bf16[128,8,128]{2,0,1:T(8,128)(2,1)S(1)} all-to-all(bf16[128,8,128]{2,0,1:T(8,128)(2,1)S(1)} %copy.30), channel_id=1, replica_groups=mesh['seq'=32,'head'=8] {'head'}, dimensions={1} | all-to-all | bytes 524288 | tf_op jit(solution)/shard_map/all_to_all | solution.py:52
  40.0 5.1 %stack.5 = bf16[32,1024,1,128]{3,1,2,0:T(8,128)(2,1)} broadcast(bf16[1024,128]{1,0:T(8,128)(2,1)S(1)} %bitcast.122), dimensions={1,3} | broadcast | bytes 8650752 | tf_op jit(solution)/shard_map/stack | solution.py:46
  45.1 10.6 %all-to-all-start.2 = ((bf16[32,1024,1,128]{3,1,2,0:T(8,128)(2,1)}), bf16[32,1024,1,128]{3,1,2,0:T(8,128)(2,1)}, u32[]{:S(2)}, u32[]{:S(2)}) async-start(bf16[32,1024,1,128]{3,1,2,0:T(8,128)(2,1)} %stack.5), calls=%async_computation.2 | async-start | bytes 16777216 | tf_op jit(solution)/shard_map/all_to_all | solution.py:47
  55.7 2.7 copy.32
  58.4 113.3 %all-to-all-done.2 = bf16[32,1024,1,128]{3,1,2,0:T(8,128)(2,1)} async-done(((bf16[32,1024,1,128]{3,1,2,0:T(8,128)(2,1)}), bf16[32,1024,1,128]{3,1,2,0:T(8,128)(2,1)}, u32[]{:S(2)}, u32[]{:S(2)}) %all-to-all-start.2) | async-done | bytes 8388640 | tf_op jit(solution)/shard_map/all_to_all | solution.py:47
  171.6 4.3 %all-to-all-start.3 = ((bf16[128,64,128]{2,0,1:T(8,128)(2,1)}), bf16[128,64,128]{2,0,1:T(8,128)(2,1)}, u32[]{:S(2)}, u32[]{:S(2)}) async-start(bf16[128,64,128]{2,0,1:T(8,128)(2,1)} %copy.32), calls=%async_computation.3 | async-start | bytes 4194304 | tf_op jit(solution)/shard_map/all_to_all | solution.py:51
  176.1 0.8 gather_fusion
  177.1 4.3 %gather_fusion.2 = bf16[64,128,128]{2,1,0:T(8,128)(2,1)S(1)} fusion(bf16[256,128,128]{2,1,0:T(8,128)(2,1)} %bitcast.29, s32[1024]{0:T(1024)S(1)} %pad_clamp_fusion), kind=kCustom, calls=%fused_computation.1.clone | custom fusion | bytes 4194560 | tf_op jit(solution)/shard_map/jit(_take)/gather | solution.py:67
  181.4 1.6 broadcast_select_fusion
  183.1 4.3 %gather_fusion.1 = bf16[64,128,128]{2,1,0:T(8,128)(2,1)S(1)} fusion(bf16[256,128,128]{2,1,0:T(8,128)(2,1)} %bitcast.126, s32[1024]{0:T(1024)S(1)} %pad_clamp_fusion), kind=kCustom, calls=%fused_computation.clone | custom fusion | bytes 4194560 | tf_op jit(solution)/shard_map/jit(_take)/gather | solution.py:68
  187.4 1.6 select_bitcast_fusion
  189.0 37.6 %all-to-all-done.3 = bf16[128,64,128]{2,0,1:T(8,128)(2,1)} async-done(((bf16[128,64,128]{2,0,1:T(8,128)(2,1)}), bf16[128,64,128]{2,0,1:T(8,128)(2,1)}, u32[]{:S(2)}, u32[]{:S(2)}) %all-to-all-start.3) | async-done | bytes 2097184 | tf_op jit(solution)/shard_map/all_to_all | solution.py:51
  226.5 67.0 %while.10 = (s32[]{:T(128)}, bf16[8,128,1,8,128]{4,3,1,0,2:T(8,128)(2,1)}, bf16[8,128,1,128]{3,1,0,2:T(8,128)(2,1)}, bf16[8,8,128,1,128]{4,2,1,3,0:T(8,128)(2,1)...) while((s32[]{:T(128)}, ...), condition=%wide.region_3.5_spmd, body=%wide.region_0.4_spmd.sunk | while | flops 616381568 | bytes 19326696 | solution.py:72
  226.5 1.1 dynamic-slice_bitcast_fusion.3
  227.6 0.8 constant_dynamic-slice_fusion.4
  230.1 1.8 fusion.34
  231.9 0.8 fusion.35
  232.7 1.3 fusion.36
  234.2 0.7 constant_dynamic-update-slice_fusion.2
  234.9 1.1 dynamic-slice_bitcast_fusion.3
  236.0 0.8 constant_dynamic-slice_fusion.4
  238.5 1.8 fusion.34
  240.2 0.8 fusion.35
  241.1 1.3 fusion.36
  242.6 0.7 constant_dynamic-update-slice_fusion.2
  243.3 1.1 dynamic-slice_bitcast_fusion.3
  244.4 0.8 constant_dynamic-slice_fusion.4
  246.8 1.8 fusion.34
  248.6 0.8 fusion.35
  249.5 1.3 fusion.36
  250.9 0.7 constant_dynamic-update-slice_fusion.2
  251.7 1.1 dynamic-slice_bitcast_fusion.3
  252.7 0.8 constant_dynamic-slice_fusion.4
  255.2 1.8 fusion.34
  257.0 0.8 fusion.35
  257.8 1.3 fusion.36
  259.3 0.7 constant_dynamic-update-slice_fusion.2
  260.0 1.1 dynamic-slice_bitcast_fusion.3
  261.1 0.8 constant_dynamic-slice_fusion.4
  263.6 1.8 fusion.34
  265.4 0.8 fusion.35
  266.2 1.3 fusion.36
  267.7 0.7 constant_dynamic-update-slice_fusion.2
  268.4 1.1 dynamic-slice_bitcast_fusion.3
  269.5 0.8 constant_dynamic-slice_fusion.4
  271.9 1.8 fusion.34
  273.7 0.8 fusion.35
  274.6 1.3 fusion.36
  276.8 1.1 dynamic-slice_bitcast_fusion.3
  277.8 0.8 constant_dynamic-slice_fusion.4
  280.3 1.8 fusion.34
  282.1 0.8 fusion.35
  283.0 1.3 fusion.36
  285.1 1.1 dynamic-slice_bitcast_fusion.3
  286.2 0.8 constant_dynamic-slice_fusion.4
  288.7 1.8 fusion.34
  290.5 0.8 fusion.35
  291.3 1.3 fusion.36
  292.8 0.7 constant_dynamic-update-slice_fusion.2
  293.5 55.1 %all_to_all.73 = bf16[1024,8,128]{2,1,0:T(8,128)(2,1)S(1)} all-to-all(bf16[1024,8,128]{2,1,0:T(8,128)(2,1)} %bitcast.121), channel_id=1, replica_groups=mesh['seq'=32,'head'=8] {'head'}, dimensions={0} | all-to-all | bytes 4194304 | tf_op jit(solution)/shard_map/all_to_all | solution.py:77
  348.6 1.9 copy.42
  (98 shorter events, 16.9 us)
Async XLA Ops:
  6.5 176.5 %all-gather.2.cloned.1.call-start = ((), (), s32[]{:S(2)}) async-start(), calls=%async_computation.5 | async-start | bytes 8650752 | tf_op jit(solution)/shard_map/all_gather | solution.py:63
  45.1 10.6 %copy-start.1 = (bf16[128,64,128]{2,1,0:T(8,128)(2,1)S(1)}, bf16[128,64,128]{2,1,0:T(8,128)(2,1)}, u32[]{:S(2)}) copy-start(bf16[128,64,128]{2,1,0:T(8,128)(2,1)} %param.9) | copy-start | bytes 6291460
  45.1 126.5 %all-to-all-start.2 = ((bf16[32,1024,1,128]{3,1,2,0:T(8,128)(2,1)}), bf16[32,1024,1,128]{3,1,2,0:T(8,128)(2,1)}, u32[]{:S(2)}, u32[]{:S(2)}) async-start(bf16[32,1024,1,128]{3,1,2,0:T(8,128)(2,1)} %stack.5), calls=%async_computation.2 | async-start | bytes 16777216 | tf_op jit(solution)/shard_map/all_to_all | solution.py:47
  58.4 117.6 %copy-start.2 = (s32[8,8]{1,0:T(8,128)S(1)}, s32[8,8]{1,0:T(8,128)}, u32[]{:S(2)}) copy-start(s32[8,8]{1,0:T(8,128)} %param.12) | copy-start | bytes 772
  58.4 117.7 %copy-start = (s32[256]{0:T(256)S(1)}, s32[256]{0:T(256)}, u32[]{:S(2)}) copy-start(s32[256]{0:T(256)} %param.13) | copy-start | bytes 3076
  171.6 54.9 %all-to-all-start.3 = ((bf16[128,64,128]{2,0,1:T(8,128)(2,1)}), bf16[128,64,128]{2,0,1:T(8,128)(2,1)}, u32[]{:S(2)}, u32[]{:S(2)}) async-start(bf16[128,64,128]{2,0,1:T(8,128)(2,1)} %copy.32), calls=%async_computation.3 | async-start | bytes 4194304 | tf_op jit(solution)/shard_map/all_to_all | solution.py:51
Sparse Core Ops, SparseCore 0:
  27.1 140.8 all-gather.1
